TPU v7x, 32 devices: a whole 2x2x4 slice. The times are simulated.
32 devices in a mesh: tm: 8 (over z, x), rows: 4 (over y, core).
Axes of the slice: x: 2, y: 2, z: 4, core: 2. Of those that a mesh axis runs over, the one named last changes fastest.
Arguments:
- latents: bfloat16 [32, 16, 32, 256], P('tm', 'rows'), may hold values from -6 to 6
- frame_gaps: float32 [32], P('tm'), may hold values from 0.5 to 250
- decay_rates: float32 [2, 256], replicated, may hold values from 0.0011 to 0.05
- input_kernel: bfloat16 [2, 3, 3, 256, 256], replicated, may hold values from -0.125 to 0.125
- output_kernel: bfloat16 [2, 3, 3, 256, 256], replicated, may hold values from -0.125 to 0.125
- feedthrough: float32 [2, 256], replicated, may hold values from -1 to 1
Outputs:
- encoded: bfloat16 [32, 16, 32, 256], P('tm', 'rows')
All inputs are finite; a program needn't handle non-finite values.
Results may differ from a plain program's by a relative error of at most 0.012.
Values may be sent and summed in bfloat16 or wider, within the bound.
A program may use at most 64 MiB of HBM per device.

v0:
```python
import functools

import jax
import jax.numpy as jnp
from jax import lax
from jax.experimental import pallas as pl
from jax.experimental.pallas import tpu as pltpu
from jax.sharding import PartitionSpec as P

MESH = pl.DeviceIdType.MESH
F32 = jnp.float32
BF16 = jnp.bfloat16


def gelu(v):
    return 0.5 * v * (1.0 + jnp.tanh(0.7978845608028654 * (v + 0.044715 * (v * v * v))))


def fold(v):
    half = v.shape[-1] // 2
    return jnp.concatenate([v[..., :half], v[..., half:]], axis=-2)


def unfold(v):
    half = v.shape[-2] // 2
    return jnp.concatenate([v[..., :half, :], v[..., half:, :]], axis=-1)


def kernel(
    n, bands, base, owners,
    lat, gaps_in, rates_in, feed_in, win, wout,
    out,
    gaps, rates, feed, x0, x1, xs, xh, st, sth, halo, wbuf, cums, dec_src, dec_box,
    fin, inbox, xbox, outbox, carry, hcarry,
    small_sem, lat_sem, w_sem, halo_send, halo_recv, dec_send, dec_recv, fin_send, fin_recv, cross_send, cross_recv,
    car_send, car_recv, hcar_send, hcar_recv,
):
    layers = win.shape[0]
    frames, rows, width, chans = lat.shape
    share = width // owners
    me = lax.axis_index("tm")
    band = lax.axis_index("rows")
    has_up = band > 0
    has_down = band < bands - 1
    is_owner = jnp.logical_and(me >= base, me < base + owners)
    my_share = lax.rem(me + owners * n - base, owners)
    groups = [list(range(rows // 2)), list(range(rows // 2, rows))]
    sides = [(has_up, lax.rem(band + bands - 1, bands)), (has_down, lax.rem(band + 1, bands))]
    beyond_row = [-1, rows]
    edge_row = [0, rows - 1]
    pending = []

    def both(*conds):
        return functools.reduce(jnp.logical_and, conds)

    def send(cond, src, dst, ssem, rsem, dev):
        copy = pltpu.make_async_remote_copy(
            src_ref=src, dst_ref=dst, send_sem=ssem, recv_sem=rsem, device_id=dev, device_id_type=MESH
        )
        pl.when(cond)(copy.start)
        pending.append((cond, copy))

    def receive(cond, dst, ssem, rsem, dev):
        copy = pltpu.make_async_remote_copy(
            src_ref=dst, dst_ref=dst, send_sem=ssem, recv_sem=rsem, device_id=dev, device_id_type=MESH
        )
        pl.when(cond)(copy.wait_recv)

    barrier = pltpu.get_barrier_semaphore()

    def greet(cond, dev):
        @pl.when(cond)
        def _():
            pl.semaphore_signal(barrier, inc=1, device_id=dev, device_id_type=MESH)

    small = [pltpu.make_async_copy(src, dst, small_sem.at[i])
             for i, (src, dst) in enumerate(((gaps_in, gaps), (rates_in, rates), (feed_in, feed)))]
    w_copies = {(layer, which): pltpu.make_async_copy(src.at[layer], wbuf.at[layer, which], w_sem.at[layer, which])
                for layer in range(layers) for which, src in enumerate((win, wout))}
    row_copies = [pltpu.make_async_copy(lat.at[:, r], x0.at[r], lat_sem.at[r]) for r in range(rows)]

    for k in range(n):
        owns = base <= k < base + owners
        greet(me != k if owns else both(is_owner, me != k), {"tm": k})
    for copy in small:
        copy.start()
    w_copies[0, 0].start()
    for copy in row_copies:
        copy.start()
    for there, other in sides:
        for k in range(n):
            if base <= k < base + owners:
                greet(there, {"tm": k, "rows": other})
            else:
                greet(both(there, jnp.logical_or(is_owner, me == k)), {"tm": k, "rows": other})

    for d, (there, _other) in enumerate(sides):
        @pl.when(jnp.logical_not(there))
        def _():
            for layer in range(layers):
                for which in range(2):
                    halo[layer, which, d] = jnp.zeros(halo.shape[3:], BF16)
                xbox[layer, d] = jnp.zeros(xbox.shape[2:], BF16)

        @pl.when(jnp.logical_or(me == 0, jnp.logical_not(there)))
        def _():
            for layer in range(layers):
                hcarry[layer, d] = jnp.zeros(hcarry.shape[2:], BF16)

    @pl.when(me == 0)
    def _():
        carry[...] = jnp.zeros(carry.shape, BF16)

    for copy in small:
        copy.wait()
    decays = []
    for layer in range(layers):
        rate = rates[layer : layer + 1, :]
        factors = [jnp.exp(-gaps[t] * rate) for t in range(frames)]
        total = factors[0]
        cums[layer, 0:1, :] = total
        for t in range(1, frames):
            total = total * factors[t]
            cums[layer, t : t + 1, :] = total
        dec_src[layer : layer + 1, :] = total
        decays.append([(factor, jnp.sqrt(1.0 - factor * factor)) for factor in factors])

    @pl.when(is_owner)
    def _():
        dec_box[me] = dec_src[...]

    neighbours = has_up.astype(jnp.int32) + has_down.astype(jnp.int32)

    def meet():
        pl.semaphore_wait(
            barrier, jnp.where(is_owner, n - 1 + neighbours * n, owners + neighbours * (owners + 1))
        )

    def send_halo(layer, which, top, bottom):
        for d, (src, (there, other)) in enumerate(zip((top, bottom), sides)):
            send(there, src, halo.at[layer, which, 1 - d], halo_send.at[layer, which, d],
                 halo_recv.at[layer, which, 1 - d], {"rows": other})

    def wait_halo(layer, which):
        for d, (there, other) in enumerate(sides):
            receive(there, halo.at[layer, which, d], halo_send.at[layer, which, d],
                    halo_recv.at[layer, which, d], {"rows": other})

    def spread(parts, count):
        size = count * frames * width
        column = lax.rem(lax.broadcasted_iota(jnp.int32, (size, parts[0].shape[1]), 0), width)
        left = jnp.where(column == 0, 0.0, pltpu.roll(parts[0], 1, 0))
        right = jnp.where(column == width - 1, 0.0, pltpu.roll(parts[2], size - 1, 0))
        return (parts[1] + left + right).reshape(count, frames, width, -1)

    def conv(x, weights, wanted):
        lhs = [jnp.concatenate([x(i + a - 1).reshape(frames * width, chans) for i in wanted], axis=0) for a in range(3)]
        lhs = jnp.concatenate(lhs, axis=1)
        parts = []
        for b in range(3):
            rhs = jnp.concatenate([weights(a, b) for a in range(3)], axis=0)
            parts.append(jnp.dot(lhs, rhs, preferred_element_type=F32))
        return spread(parts, len(wanted))

    def scan(layer, driven):
        states = []
        for t in range(frames):
            factor, gain = decays[layer][t]
            fresh = gain * driven[t]
            states.append(fresh if t == 0 else factor * states[-1] + fresh)
        return states

    def drive(x, layer, g):
        mine = groups[g]
        wanted = [-1] + mine if g == 0 else mine + [rows]
        nothing = jnp.zeros((frames, width, chans), BF16)
        driven = conv(lambda i: x(i) if 0 <= i < rows else nothing, lambda a, b: wbuf[layer, 0, a, b], wanted)
        for j, r in enumerate(wanted):
            states = scan(layer, driven[j])
            if 0 <= r < rows:
                for t in range(frames):
                    st[r, t] = states[t]
            slot = r - mine[0] if 0 <= r < rows else len(mine)
            for s in range(owners):
                fin[layer, g, s, slot] = fold(states[-1][s * share : (s + 1) * share]).astype(BF16)

    def send_fin(layer, g):
        count = len(groups[g])
        there, other = sides[g]
        for s in range(owners):
            @pl.when(me == base + s)
            def _():
                inbox[layer, g, me, :count] = fin[layer, g, s, :count]

            send(both(me < n - 1, there), fin.at[layer, g, s, count], xbox.at[layer, 1 - g, me],
                 cross_send.at[layer, g, s], cross_recv.at[layer, 1 - g, me], {"tm": base + s, "rows": other})
            send(both(me < n - 1, me != base + s), fin.at[layer, g, s, :count], inbox.at[layer, g, me, :count],
                 fin_send.at[layer, g, s], fin_recv.at[layer, g, me], {"tm": base + s})

    def own(layer, g):
        count = len(groups[g])
        there, other = sides[g]
        edge = 0 if g == 0 else count - 1
        total = None
        for k in range(1, n):
            receive(both(is_owner, me != k - 1), inbox.at[layer, g, k - 1, :count], fin_send.at[layer, g, 0],
                    fin_recv.at[layer, g, k - 1], {"tm": k - 1})
            receive(both(is_owner, there), xbox.at[layer, g, k - 1], cross_send.at[layer, g, 0],
                    cross_recv.at[layer, g, k - 1], {"tm": k - 1, "rows": other})
            if layer == 0 and g == 0:
                receive(both(is_owner, me != k - 1), dec_box.at[k - 1], dec_send.at[0], dec_recv.at[k - 1], {"tm": k - 1})
            last = unfold(inbox[layer, g, k - 1, :count].astype(F32))
            cross = unfold(xbox[layer, g, k - 1].astype(F32))
            last = jnp.stack([last[j] + cross if j == edge else last[j] for j in range(count)])
            total = last if total is None else dec_box[k - 1, layer : layer + 1, :] * total + last
            outbox[layer, g, k, :count] = fold(total).astype(BF16)
            send(both(is_owner, there), outbox.at[layer, g, k, edge], hcarry.at[layer, 1 - g, my_share],
                 hcar_send.at[layer, g, k], hcar_recv.at[layer, 1 - g, my_share], {"tm": k, "rows": other})
            send(both(is_owner, me != k), outbox.at[layer, g, k, :count], carry.at[layer, g, my_share, :count],
                 car_send.at[layer, g, k], car_recv.at[layer, g, my_share], {"tm": k})

            @pl.when(both(is_owner, me == k))
            def _():
                carry[layer, g, my_share, :count] = outbox[layer, g, k, :count]

    def complete(layer):
        wait_halo(layer, 0)
        for d in range(2):
            v = halo[layer, 0, d].reshape(frames * width, chans)
            parts = [jnp.dot(v, wbuf[layer, 0, 2 * d, b], preferred_element_type=F32) for b in range(3)]
            states = scan(layer, spread(parts, 1)[0])
            for t in range(frames):
                state = st[edge_row[d], t] + states[t]
                st[edge_row[d], t] = state
                sth[layer, d, t] = state.astype(BF16)
        send_halo(layer, 1, sth.at[layer, 0], sth.at[layer, 1])

    def finish(layer, g):
        count = len(groups[g])
        for s in range(owners):
            receive(both(me > 0, me != base + s), carry.at[layer, g, s, :count], car_send.at[layer, g, 0],
                    car_recv.at[layer, g, s], {"tm": base + s})
        for j, r in enumerate(groups[g]):
            incoming = jnp.concatenate([unfold(carry[layer, g, s, j].astype(F32)) for s in range(owners)], axis=0)
            for t in range(frames):
                xs[layer, r, t] = (st[r, t] + cums[layer, t : t + 1, :] * incoming).astype(BF16)

    def finish_halo(layer):
        wait_halo(layer, 1)
        for d, (there, other) in enumerate(sides):
            for s in range(owners):
                receive(both(me > 0, there), hcarry.at[layer, d, s], hcar_send.at[layer, d, 0],
                        hcar_recv.at[layer, d, s], {"tm": base + s, "rows": other})
            incoming = jnp.concatenate([unfold(hcarry[layer, d, s].astype(F32)) for s in range(owners)], axis=0)
            for t in range(frames):
                local = halo[layer, 1, d, t].astype(F32)
                xh[layer, d, t] = (local + cums[layer, t : t + 1, :] * incoming).astype(BF16)

    def mix(x, layer, wanted, put):
        def states(i):
            return xh[layer, 0] if i < 0 else xh[layer, 1] if i == rows else xs[layer, i]

        mixed = conv(states, lambda a, b: wbuf[layer, 1, a, b], wanted)
        gain = feed[layer : layer + 1, :]
        for j, r in enumerate(wanted):
            skipped = x(r).astype(F32)
            put(r, gelu(mixed[j] + gain * skipped).astype(BF16))

    x = lambda r: x0[r]
    for copy in row_copies:
        copy.wait()
    for layer in range(layers):
        if layer == 0:
            w_copies[0, 0].wait()
            w_copies[0, 1].start()
            drive(x, layer, 0)
            meet()
            send_halo(0, 0, lat.at[:, 0], lat.at[:, rows - 1])
            for s in range(owners):
                send(both(me < n - 1, me != base + s), dec_src, dec_box.at[me], dec_send.at[s],
                     dec_recv.at[me], {"tm": base + s})
            send_fin(layer, 0)
        else:
            w_copies[layer, 0].wait()
            send_halo(layer, 0, x1.at[layer - 1, 0], x1.at[layer - 1, rows - 1])
            drive(x, layer, 0)
            send_fin(layer, 0)
        drive(x, layer, 1)
        send_fin(layer, 1)
        if layer < layers - 1:
            w_copies[layer + 1, 0].start()
            w_copies[layer + 1, 1].start()
        complete(layer)
        for g in range(2):
            own(layer, g)
        for g in range(2):
            finish(layer, g)
        finish_halo(layer)
        w_copies[layer, 1].wait()
        if layer == layers - 1:
            def put(r, v):
                out[:, r] = v
        else:
            def put(r, v):
                x1[layer, r] = v

        mix(x, layer, list(range(rows)), put)
        x = functools.partial(lambda layer, r: x1[layer, r], layer)

    for cond, copy in pending:
        pl.when(cond)(copy.wait_send)


def per_device(n, bands, latents, frame_gaps, decay_rates, input_kernel, output_kernel, feedthrough):
    frames, rows, width, chans = latents.shape
    layers = input_kernel.shape[0]
    owners = min(n // 2, max(width // 8, 1))
    base = n // 2 - owners // 2
    share = width // owners
    most = rows - rows // 2
    hbm = pl.BlockSpec(memory_space=pltpu.HBM)
    vmem = pl.BlockSpec(memory_space=pltpu.VMEM)
    dma = pltpu.SemaphoreType.DMA
    return pl.pallas_call(
        functools.partial(kernel, n, bands, base, owners),
        out_shape=pltpu.VMEM(latents.shape, BF16),
        in_specs=[hbm] * 6,
        out_specs=vmem,
        scratch_shapes=[
            pltpu.SMEM((frames,), F32),
            pltpu.VMEM((layers, chans), F32),
            pltpu.VMEM((layers, chans), F32),
            pltpu.VMEM((rows, frames, width, chans), BF16),
            pltpu.VMEM((max(layers - 1, 1), rows, frames, width, chans), BF16),
            pltpu.VMEM((layers, rows, frames, width, chans), BF16),
            pltpu.VMEM((layers, 2, frames, width, chans), BF16),
            pltpu.VMEM((rows, frames, width, chans), F32),
            pltpu.VMEM((layers, 2, frames, width, chans), BF16),
            pltpu.VMEM((layers, 2, 2, frames, width, chans), BF16),
            pltpu.VMEM((layers, 2) + input_kernel.shape[1:], BF16),
            pltpu.VMEM((layers, frames, chans), F32),
            pltpu.VMEM((layers, chans), F32),
            pltpu.VMEM((n, layers, chans), F32),
            pltpu.VMEM((layers, 2, owners, most + 1, 2 * share, chans // 2), BF16),
            pltpu.VMEM((layers, 2, n, most, 2 * share, chans // 2), BF16),
            pltpu.VMEM((layers, 2, n, 2 * share, chans // 2), BF16),
            pltpu.VMEM((layers, 2, n, most, 2 * share, chans // 2), BF16),
            pltpu.VMEM((layers, 2, owners, most, 2 * share, chans // 2), BF16),
            pltpu.VMEM((layers, 2, owners, 2 * share, chans // 2), BF16),
            dma((3,)),
            dma((rows,)),
            dma((layers, 2)),
            dma((layers, 2, 2)),
            dma((layers, 2, 2)),
            dma((owners,)),
            dma((n,)),
            dma((layers, 2, owners)),
            dma((layers, 2, n)),
            dma((layers, 2, owners)),
            dma((layers, 2, n)),
            dma((layers, 2, n)),
            dma((layers, 2, owners)),
            dma((layers, 2, n)),
            dma((layers, 2, owners)),
        ],
        compiler_params=pltpu.CompilerParams(collective_id=0, has_side_effects=True, vmem_limit_bytes=60 * 1024 * 1024),
    )(latents, frame_gaps, decay_rates, feedthrough, input_kernel, output_kernel)


def solution(mesh):
    in_specs = (P("tm", "rows", None, None), P("tm"), P(), P(), P(), P())
    out_specs = P("tm", "rows", None, None)
    return jax.shard_map(
        functools.partial(per_device, mesh.shape["tm"], mesh.shape["rows"]),
        mesh=mesh, in_specs=in_specs, out_specs=out_specs, check_vma=False,
    )
```

profile of v0, /device:TPU:6, one launch (start us, length us, event | category | flops | bytes accessed | tf_op | source)
XLA Modules:
  0.0 26.2 jit_solution(9147007909175763055)
XLA Ops:
  0.0 25.5 %shard_map.64 = bf16[4,4,32,256]{3,2,1,0:T(8,128)(2,1)S(1)} custom-call(bf16[4,4,32,256]{3,2,1,0:T(8,128)(2,1)} %lat.1, f32[4]{0:T(128)} %gaps_in.1, f32[2,256]{1,0:T(2,128)} %rates_in.1, f32[2,256]{1,0:T(2,128)} %feed_in.1, bf16[2,3,3,256,256]{4,3,2,1,0:T(8,128)(2,1)} %win.1, bf16[2,3,3,256,256]{4,3,2,1,0:T(8,128)(2,1)} %wout.1), custom_call_target="tpu_custom_call" | custom-call | tf_op jit(solution)/shard_map/pallas_call | solution.py:324
  25.5 0.7 %copy.8 = bf16[4,4,32,256]{3,2,1,0:T(8,128)(2,1)} copy(bf16[4,4,32,256]{3,2,1,0:T(8,128)(2,1)S(1)} %shard_map.64) | data formatting | bytes 524288
where the time goes:
time: 26.4 us; the launch traced here: 26.2 us
  Pallas kernels  25.5 us (97%)
  local copies, waits for them, and re-layouts  0.71 us (3%)
    pallas_call x1, Pallas kernels, per_device(): pl.pallas_call(functools.partial(kernel, n, bands, base, owners), out_sha...  25.5 us
    unnamed x1, local copies, waits for them, and re-layouts  0.71 us

commit v1 on v0

--- a/solution.py
+++ b/solution.py
@@ -48,7 +48,6 @@
     sides = [(has_up, lax.rem(band + bands - 1, bands)), (has_down, lax.rem(band + 1, bands))]
     beyond_row = [-1, rows]
     edge_row = [0, rows - 1]
-    pending = []
 
     def both(*conds):
         return functools.reduce(jnp.logical_and, conds)
@@ -58,13 +57,22 @@
             src_ref=src, dst_ref=dst, send_sem=ssem, recv_sem=rsem, device_id=dev, device_id_type=MESH
         )
         pl.when(cond)(copy.start)
-        pending.append((cond, copy))
-
-    def receive(cond, dst, ssem, rsem, dev):
-        copy = pltpu.make_async_remote_copy(
-            src_ref=dst, dst_ref=dst, send_sem=ssem, recv_sem=rsem, device_id=dev, device_id_type=MESH
+
+    def waiter(ref, sem):
+        return pltpu.make_async_remote_copy(
+            src_ref=ref, dst_ref=ref, send_sem=sem, recv_sem=sem, device_id={"tm": 0}, device_id_type=MESH
         )
-        pl.when(cond)(copy.wait_recv)
+
+    def received(cond, ref, sem):
+        if ref is not None:
+            pl.when(cond)(lambda: waiter(ref, sem).wait_recv())
+
+    def sent(cond, ref, sem):
+        if ref is not None:
+            pl.when(cond)(lambda: waiter(ref, sem).wait_send())
+
+    def first(ref, lead, size, *rest):
+        return ref.at[(*lead, pl.ds(0, size), *rest)] if size else None
 
     barrier = pltpu.get_barrier_semaphore()
 
@@ -77,7 +85,7 @@
              for i, (src, dst) in enumerate(((gaps_in, gaps), (rates_in, rates), (feed_in, feed)))]
     w_copies = {(layer, which): pltpu.make_async_copy(src.at[layer], wbuf.at[layer, which], w_sem.at[layer, which])
                 for layer in range(layers) for which, src in enumerate((win, wout))}
-    row_copies = [pltpu.make_async_copy(lat.at[:, r], x0.at[r], lat_sem.at[r]) for r in range(rows)]
+    row_copies = [pltpu.make_async_copy(lat.at[:, r], x0.at[r], lat_sem) for r in range(rows)]
 
     for k in range(n):
         owns = base <= k < base + owners
@@ -138,13 +146,12 @@
 
     def send_halo(layer, which, top, bottom):
         for d, (src, (there, other)) in enumerate(zip((top, bottom), sides)):
-            send(there, src, halo.at[layer, which, 1 - d], halo_send.at[layer, which, d],
+            send(there, src, halo.at[layer, which, 1 - d], halo_send.at[d],
                  halo_recv.at[layer, which, 1 - d], {"rows": other})
 
     def wait_halo(layer, which):
-        for d, (there, other) in enumerate(sides):
-            receive(there, halo.at[layer, which, d], halo_send.at[layer, which, d],
-                    halo_recv.at[layer, which, d], {"rows": other})
+        for d, (there, _other) in enumerate(sides):
+            received(there, halo.at[layer, which, d], halo_recv.at[layer, which, d])
 
     def spread(parts, count):
         size = count * frames * width
@@ -193,35 +200,35 @@
                 inbox[layer, g, me, :count] = fin[layer, g, s, :count]
 
             send(both(me < n - 1, there), fin.at[layer, g, s, count], xbox.at[layer, 1 - g, me],
-                 cross_send.at[layer, g, s], cross_recv.at[layer, 1 - g, me], {"tm": base + s, "rows": other})
+                 cross_send.at[g], cross_recv.at[layer, 1 - g], {"tm": base + s, "rows": other})
             send(both(me < n - 1, me != base + s), fin.at[layer, g, s, :count], inbox.at[layer, g, me, :count],
-                 fin_send.at[layer, g, s], fin_recv.at[layer, g, me], {"tm": base + s})
+                 fin_send.at[g], fin_recv.at[layer, g], {"tm": base + s})
 
     def own(layer, g):
         count = len(groups[g])
         there, other = sides[g]
         edge = 0 if g == 0 else count - 1
-        total = None
-        for k in range(1, n):
-            receive(both(is_owner, me != k - 1), inbox.at[layer, g, k - 1, :count], fin_send.at[layer, g, 0],
-                    fin_recv.at[layer, g, k - 1], {"tm": k - 1})
-            receive(both(is_owner, there), xbox.at[layer, g, k - 1], cross_send.at[layer, g, 0],
-                    cross_recv.at[layer, g, k - 1], {"tm": k - 1, "rows": other})
-            if layer == 0 and g == 0:
-                receive(both(is_owner, me != k - 1), dec_box.at[k - 1], dec_send.at[0], dec_recv.at[k - 1], {"tm": k - 1})
-            last = unfold(inbox[layer, g, k - 1, :count].astype(F32))
-            cross = unfold(xbox[layer, g, k - 1].astype(F32))
-            last = jnp.stack([last[j] + cross if j == edge else last[j] for j in range(count)])
-            total = last if total is None else dec_box[k - 1, layer : layer + 1, :] * total + last
-            outbox[layer, g, k, :count] = fold(total).astype(BF16)
-            send(both(is_owner, there), outbox.at[layer, g, k, edge], hcarry.at[layer, 1 - g, my_share],
-                 hcar_send.at[layer, g, k], hcar_recv.at[layer, 1 - g, my_share], {"tm": k, "rows": other})
-            send(both(is_owner, me != k), outbox.at[layer, g, k, :count], carry.at[layer, g, my_share, :count],
-                 car_send.at[layer, g, k], car_recv.at[layer, g, my_share], {"tm": k})
-
-            @pl.when(both(is_owner, me == k))
-            def _():
-                carry[layer, g, my_share, :count] = outbox[layer, g, k, :count]
+
+        @pl.when(is_owner)
+        def _():
+            for last, size in ((me < n - 1, n - 2), (me == n - 1, n - 1)):
+                received(last, first(inbox, (layer, g), size, pl.ds(0, count)), fin_recv.at[layer, g])
+                if layer == 0 and g == 0:
+                    received(last, first(dec_box, (), size), dec_recv)
+            received(there, first(xbox, (layer, g), n - 1), cross_recv.at[layer, g])
+            total = None
+            for k in range(1, n):
+                last = unfold(inbox[layer, g, k - 1, :count].astype(F32))
+                cross = unfold(xbox[layer, g, k - 1].astype(F32))
+                last = jnp.stack([last[j] + cross if j == edge else last[j] for j in range(count)])
+                total = last if total is None else dec_box[k - 1, layer : layer + 1, :] * total + last
+                outbox[layer, g, k, :count] = fold(total).astype(BF16)
+                send(there, outbox.at[layer, g, k, edge], hcarry.at[layer, 1 - g, my_share],
+                     hcar_send.at[g], hcar_recv.at[layer, 1 - g], {"tm": k, "rows": other})
+                send(me != k, outbox.at[layer, g, k, :count], carry.at[layer, g, my_share, :count],
+                     car_send.at[g], car_recv.at[layer, g], {"tm": k})
+
+            carry[layer, g, my_share, :count] = outbox[layer, g, me, :count]
 
     def complete(layer):
         wait_halo(layer, 0)
@@ -237,9 +244,8 @@
 
     def finish(layer, g):
         count = len(groups[g])
-        for s in range(owners):
-            receive(both(me > 0, me != base + s), carry.at[layer, g, s, :count], car_send.at[layer, g, 0],
-                    car_recv.at[layer, g, s], {"tm": base + s})
+        for cond, size in ((is_owner, owners - 1), (jnp.logical_not(is_owner), owners)):
+            received(both(me > 0, cond), first(carry, (layer, g), size, pl.ds(0, count)), car_recv.at[layer, g])
         for j, r in enumerate(groups[g]):
             incoming = jnp.concatenate([unfold(carry[layer, g, s, j].astype(F32)) for s in range(owners)], axis=0)
             for t in range(frames):
@@ -247,10 +253,8 @@
 
     def finish_halo(layer):
         wait_halo(layer, 1)
-        for d, (there, other) in enumerate(sides):
-            for s in range(owners):
-                receive(both(me > 0, there), hcarry.at[layer, d, s], hcar_send.at[layer, d, 0],
-                        hcar_recv.at[layer, d, s], {"tm": base + s, "rows": other})
+        for d, (there, _other) in enumerate(sides):
+            received(both(me > 0, there), hcarry.at[layer, d], hcar_recv.at[layer, d])
             incoming = jnp.concatenate([unfold(hcarry[layer, d, s].astype(F32)) for s in range(owners)], axis=0)
             for t in range(frames):
                 local = halo[layer, 1, d, t].astype(F32)
@@ -267,8 +271,7 @@
             put(r, gelu(mixed[j] + gain * skipped).astype(BF16))
 
     x = lambda r: x0[r]
-    for copy in row_copies:
-        copy.wait()
+    pltpu.make_async_copy(x0, x0, lat_sem).wait()
     for layer in range(layers):
         if layer == 0:
             w_copies[0, 0].wait()
@@ -277,8 +280,8 @@
             meet()
             send_halo(0, 0, lat.at[:, 0], lat.at[:, rows - 1])
             for s in range(owners):
-                send(both(me < n - 1, me != base + s), dec_src, dec_box.at[me], dec_send.at[s],
-                     dec_recv.at[me], {"tm": base + s})
+                send(both(me < n - 1, me != base + s), dec_src, dec_box.at[me], dec_send,
+                     dec_recv, {"tm": base + s})
             send_fin(layer, 0)
         else:
             w_copies[layer, 0].wait()
@@ -307,8 +310,15 @@
         mix(x, layer, list(range(rows)), put)
         x = functools.partial(lambda layer, r: x1[layer, r], layer)
 
-    for cond, copy in pending:
-        pl.when(cond)(copy.wait_send)
+    for cond, size in ((is_owner, owners - 1), (jnp.logical_not(is_owner), owners)):
+        sent(both(me < n - 1, cond), first(dec_box, (), size), dec_send)
+        for g in range(2):
+            sent(both(me < n - 1, cond), first(fin, (slice(None), g), size, pl.ds(0, len(groups[g]))), fin_send.at[g])
+    for g, (there, _other) in enumerate(sides):
+        sent(there, halo.at[:, :, g], halo_send.at[g])
+        sent(both(me < n - 1, there), fin.at[:, g, :, len(groups[g])], cross_send.at[g])
+        sent(is_owner, first(outbox, (slice(None), g), n - 2, pl.ds(0, len(groups[g]))), car_send.at[g])
+        sent(both(is_owner, there), outbox.at[:, g, pl.ds(0, n - 1), 0], hcar_send.at[g])
 
 
 def per_device(n, bands, latents, frame_gaps, decay_rates, input_kernel, output_kernel, feedthrough):
@@ -348,20 +358,20 @@
             pltpu.VMEM((layers, 2, owners, most, 2 * share, chans // 2), BF16),
             pltpu.VMEM((layers, 2, owners, 2 * share, chans // 2), BF16),
             dma((3,)),
-            dma((rows,)),
-            dma((layers, 2)),
+            dma,
+            dma((layers, 2)),
+            dma((2,)),
             dma((layers, 2, 2)),
-            dma((layers, 2, 2)),
-            dma((owners,)),
-            dma((n,)),
-            dma((layers, 2, owners)),
-            dma((layers, 2, n)),
-            dma((layers, 2, owners)),
-            dma((layers, 2, n)),
-            dma((layers, 2, n)),
-            dma((layers, 2, owners)),
-            dma((layers, 2, n)),
-            dma((layers, 2, owners)),
+            dma,
+            dma,
+            dma((2,)),
+            dma((layers, 2)),
+            dma((2,)),
+            dma((layers, 2)),
+            dma((2,)),
+            dma((layers, 2)),
+            dma((2,)),
+            dma((layers, 2)),
         ],
         compiler_params=pltpu.CompilerParams(collective_id=0, has_side_effects=True, vmem_limit_bytes=60 * 1024 * 1024),
     )(latents, frame_gaps, decay_rates, feedthrough, input_kernel, output_kernel)

time: 26.4 us -> 25.1 us (0.951)
  the two profiles are of different devices: /device:TPU:6 before, /device:TPU:3 now
where the time goes in v1:
time: 25.1 us; the launch traced here: 25 us
  Pallas kernels  24.2 us (96%)
  local copies, waits for them, and re-layouts  0.71 us (3%)
    pallas_call x1, Pallas kernels, per_device(): pl.pallas_call(functools.partial(kernel, n, bands, base, owners), out_sha...  24.2 us
    unnamed x1, local copies, waits for them, and re-layouts  0.71 us

profile of v1, /device:TPU:3, one launch (start us, length us, event | category | flops | bytes accessed | tf_op | source)
XLA Modules:
  0.0 25.0 jit_solution(13635602262428320484)
XLA Ops:
  0.0 24.2 %shard_map.64 = bf16[4,4,32,256]{3,2,1,0:T(8,128)(2,1)S(1)} custom-call(bf16[4,4,32,256]{3,2,1,0:T(8,128)(2,1)} %lat.1, f32[4]{0:T(128)} %gaps_in.1, f32[2,256]{1,0:T(2,128)} %rates_in.1, f32[2,256]{1,0:T(2,128)} %feed_in.1, bf16[2,3,3,256,256]{4,3,2,1,0:T(8,128)(2,1)} %win.1, bf16[2,3,3,256,256]{4,3,2,1,0:T(8,128)(2,1)} %wout.1), custom_call_target="tpu_custom_call" | custom-call | tf_op jit(solution)/shard_map/pallas_call | solution.py:334
  24.2 0.7 %copy.8 = bf16[4,4,32,256]{3,2,1,0:T(8,128)(2,1)} copy(bf16[4,4,32,256]{3,2,1,0:T(8,128)(2,1)S(1)} %shard_map.64) | data formatting | bytes 524288

commit v2 on v1

--- a/solution.py
+++ b/solution.py
@@ -87,14 +87,14 @@
                 for layer in range(layers) for which, src in enumerate((win, wout))}
     row_copies = [pltpu.make_async_copy(lat.at[:, r], x0.at[r], lat_sem) for r in range(rows)]
 
+    w_copies[0, 0].start()
+    for copy in small:
+        copy.start()
+    for copy in row_copies:
+        copy.start()
     for k in range(n):
         owns = base <= k < base + owners
         greet(me != k if owns else both(is_owner, me != k), {"tm": k})
-    for copy in small:
-        copy.start()
-    w_copies[0, 0].start()
-    for copy in row_copies:
-        copy.start()
     for there, other in sides:
         for k in range(n):
             if base <= k < base + owners:
@@ -169,6 +169,26 @@
             parts.append(jnp.dot(lhs, rhs, preferred_element_type=F32))
         return spread(parts, len(wanted))
 
+    def partial_conv(x, weights, wanted):
+        size = frames * width
+        blocks = {(a, i): x(i + a - 1).reshape(size, chans) for a in range(3) for i in wanted if 0 <= i + a - 1 < rows}
+        full = [i for i in wanted if all((a, i) in blocks for a in range(3))]
+        parts = []
+        for b in range(3):
+            made = {}
+            for i in wanted:
+                taps = tuple(a for a in range(3) if (a, i) in blocks)
+                made.setdefault(taps, []).append(i)
+            rows_of = {}
+            for taps, which in made.items():
+                lhs = jnp.concatenate([jnp.concatenate([blocks[a, i] for i in which], axis=0) for a in taps], axis=1)
+                rhs = jnp.concatenate([weights(a, b) for a in taps], axis=0)
+                got = jnp.dot(lhs, rhs, preferred_element_type=F32)
+                for j, i in enumerate(which):
+                    rows_of[i] = got[j * size : (j + 1) * size]
+            parts.append(jnp.concatenate([rows_of[i] for i in wanted], axis=0))
+        return spread(parts, len(wanted))
+
     def scan(layer, driven):
         states = []
         for t in range(frames):
@@ -180,8 +200,7 @@
     def drive(x, layer, g):
         mine = groups[g]
         wanted = [-1] + mine if g == 0 else mine + [rows]
-        nothing = jnp.zeros((frames, width, chans), BF16)
-        driven = conv(lambda i: x(i) if 0 <= i < rows else nothing, lambda a, b: wbuf[layer, 0, a, b], wanted)
+        driven = partial_conv(x, lambda a, b: wbuf[layer, 0, a, b], wanted)
         for j, r in enumerate(wanted):
             states = scan(layer, driven[j])
             if 0 <= r < rows:
@@ -277,6 +296,7 @@
             w_copies[0, 0].wait()
             w_copies[0, 1].start()
             drive(x, layer, 0)
+            drive(x, layer, 1)
             meet()
             send_halo(0, 0, lat.at[:, 0], lat.at[:, rows - 1])
             for s in range(owners):
@@ -288,7 +308,7 @@
             send_halo(layer, 0, x1.at[layer - 1, 0], x1.at[layer - 1, rows - 1])
             drive(x, layer, 0)
             send_fin(layer, 0)
-        drive(x, layer, 1)
+            drive(x, layer, 1)
         send_fin(layer, 1)
         if layer < layers - 1:
             w_copies[layer + 1, 0].start()

time: 25.1 us -> 25.1 us (level)
  no operation moved by 1% of the time
where the time goes in v2:
time: 25.1 us; the launch traced here: 25 us
  Pallas kernels  24.2 us (96%)
  local copies, waits for them, and re-layouts  0.71 us (3%)
    pallas_call x1, Pallas kernels, per_device(): pl.pallas_call(functools.partial(kernel, n, bands, base, owners), out_sha...  24.2 us
    unnamed x1, local copies, waits for them, and re-layouts  0.71 us

profile of v2, /device:TPU:3, one launch (start us, length us, event | category | flops | bytes accessed | tf_op | source)
XLA Modules:
  0.0 25.0 jit_solution(6065505860938198385)
XLA Ops:
  0.0 24.2 %shard_map.64 = bf16[4,4,32,256]{3,2,1,0:T(8,128)(2,1)S(1)} custom-call(bf16[4,4,32,256]{3,2,1,0:T(8,128)(2,1)} %lat.1, f32[4]{0:T(128)} %gaps_in.1, f32[2,256]{1,0:T(2,128)} %rates_in.1, f32[2,256]{1,0:T(2,128)} %feed_in.1, bf16[2,3,3,256,256]{4,3,2,1,0:T(8,128)(2,1)} %win.1, bf16[2,3,3,256,256]{4,3,2,1,0:T(8,128)(2,1)} %wout.1), custom_call_target="tpu_custom_call" | custom-call | tf_op jit(solution)/shard_map/pallas_call | solution.py:354
  24.2 0.7 %copy.8 = bf16[4,4,32,256]{3,2,1,0:T(8,128)(2,1)} copy(bf16[4,4,32,256]{3,2,1,0:T(8,128)(2,1)S(1)} %shard_map.64) | data formatting | bytes 524288

commit v3 on v1

--- a/solution.py
+++ b/solution.py
@@ -278,18 +278,20 @@
             w_copies[0, 1].start()
             drive(x, layer, 0)
             meet()
-            send_halo(0, 0, lat.at[:, 0], lat.at[:, rows - 1])
             for s in range(owners):
                 send(both(me < n - 1, me != base + s), dec_src, dec_box.at[me], dec_send,
                      dec_recv, {"tm": base + s})
             send_fin(layer, 0)
         else:
             w_copies[layer, 0].wait()
-            send_halo(layer, 0, x1.at[layer - 1, 0], x1.at[layer - 1, rows - 1])
             drive(x, layer, 0)
             send_fin(layer, 0)
         drive(x, layer, 1)
         send_fin(layer, 1)
+        if layer == 0:
+            send_halo(0, 0, lat.at[:, 0], lat.at[:, rows - 1])
+        else:
+            send_halo(layer, 0, x1.at[layer - 1, 0], x1.at[layer - 1, rows - 1])
         if layer < layers - 1:
             w_copies[layer + 1, 0].start()
             w_copies[layer + 1, 1].start()

time: 25.1 us -> 25.1 us (level)
  no operation moved by 1% of the time
where the time goes in v3:
time: 25.1 us; the launch traced here: 25 us
  Pallas kernels  24.3 us (97%)
  local copies, waits for them, and re-layouts  0.71 us (3%)
    pallas_call x1, Pallas kernels, per_device(): pl.pallas_call(functools.partial(kernel, n, bands, base, owners), out_sha...  24.3 us
    unnamed x1, local copies, waits for them, and re-layouts  0.71 us

profile of v3, /device:TPU:3, one launch (start us, length us, event | category | flops | bytes accessed | tf_op | source)
XLA Modules:
  0.0 25.0 jit_solution(12147609713819719946)
XLA Ops:
  0.0 24.3 %shard_map.64 = bf16[4,4,32,256]{3,2,1,0:T(8,128)(2,1)S(1)} custom-call(bf16[4,4,32,256]{3,2,1,0:T(8,128)(2,1)} %lat.1, f32[4]{0:T(128)} %gaps_in.1, f32[2,256]{1,0:T(2,128)} %rates_in.1, f32[2,256]{1,0:T(2,128)} %feed_in.1, bf16[2,3,3,256,256]{4,3,2,1,0:T(8,128)(2,1)} %win.1, bf16[2,3,3,256,256]{4,3,2,1,0:T(8,128)(2,1)} %wout.1), custom_call_target="tpu_custom_call" | custom-call | tf_op jit(solution)/shard_map/pallas_call | solution.py:336
  24.3 0.7 %copy.8 = bf16[4,4,32,256]{3,2,1,0:T(8,128)(2,1)} copy(bf16[4,4,32,256]{3,2,1,0:T(8,128)(2,1)S(1)} %shard_map.64) | data formatting | bytes 524288

commit v4 on v3

--- a/solution.py
+++ b/solution.py
@@ -31,7 +31,7 @@
     lat, gaps_in, rates_in, feed_in, win, wout,
     out,
     gaps, rates, feed, x0, x1, xs, xh, st, sth, halo, wbuf, cums, dec_src, dec_box,
-    fin, inbox, xbox, outbox, carry, hcarry,
+    fin, inbox, xbox, tot, outbox, carry, hcarry,
     small_sem, lat_sem, w_sem, halo_send, halo_recv, dec_send, dec_recv, fin_send, fin_recv, cross_send, cross_recv,
     car_send, car_recv, hcar_send, hcar_recv,
 ):
@@ -44,6 +44,9 @@
     has_down = band < bands - 1
     is_owner = jnp.logical_and(me >= base, me < base + owners)
     my_share = lax.rem(me + owners * n - base, owners)
+    half = max(n // 2, 1)
+    spans = [(0, half), (half, n - 1)]
+    late = (me >= half).astype(jnp.int32)
     groups = [list(range(rows // 2)), list(range(rows // 2, rows))]
     sides = [(has_up, lax.rem(band + bands - 1, bands)), (has_down, lax.rem(band + 1, bands))]
     beyond_row = [-1, rows]
@@ -72,7 +75,7 @@
             pl.when(cond)(lambda: waiter(ref, sem).wait_send())
 
     def first(ref, lead, size, *rest):
-        return ref.at[(*lead, pl.ds(0, size), *rest)] if size else None
+        return ref.at[(*lead, pl.ds(0, size), *rest)] if size > 0 else None
 
     barrier = pltpu.get_barrier_semaphore()
 
@@ -200,24 +203,25 @@
                 inbox[layer, g, me, :count] = fin[layer, g, s, :count]
 
             send(both(me < n - 1, there), fin.at[layer, g, s, count], xbox.at[layer, 1 - g, me],
-                 cross_send.at[g], cross_recv.at[layer, 1 - g], {"tm": base + s, "rows": other})
+                 cross_send.at[g], cross_recv.at[layer, 1 - g, late], {"tm": base + s, "rows": other})
             send(both(me < n - 1, me != base + s), fin.at[layer, g, s, :count], inbox.at[layer, g, me, :count],
-                 fin_send.at[g], fin_recv.at[layer, g], {"tm": base + s})
-
-    def own(layer, g):
+                 fin_send.at[g], fin_recv.at[layer, g, late], {"tm": base + s})
+
+    def own(layer, g, part):
         count = len(groups[g])
         there, other = sides[g]
         edge = 0 if g == 0 else count - 1
-
-        @pl.when(is_owner)
-        def _():
-            for last, size in ((me < n - 1, n - 2), (me == n - 1, n - 1)):
-                received(last, first(inbox, (layer, g), size, pl.ds(0, count)), fin_recv.at[layer, g])
+        low, high = spans[part]
+        inside = both(me >= low, me < high)
+
+        def gather():
+            for mine, size in ((inside, high - low - 1), (jnp.logical_not(inside), high - low)):
+                received(mine, first(inbox, (layer, g), size, pl.ds(0, count)), fin_recv.at[layer, g, part])
                 if layer == 0 and g == 0:
-                    received(last, first(dec_box, (), size), dec_recv)
-            received(there, first(xbox, (layer, g), n - 1), cross_recv.at[layer, g])
-            total = None
-            for k in range(1, n):
+                    received(mine, first(dec_box, (), size), dec_recv.at[part])
+            received(there, first(xbox, (layer, g), high - low), cross_recv.at[layer, g, part])
+            total = tot[g, :count] if part else None
+            for k in range(low + 1, high + 1):
                 last = unfold(inbox[layer, g, k - 1, :count].astype(F32))
                 cross = unfold(xbox[layer, g, k - 1].astype(F32))
                 last = jnp.stack([last[j] + cross if j == edge else last[j] for j in range(count)])
@@ -227,8 +231,12 @@
                      hcar_send.at[g], hcar_recv.at[layer, 1 - g], {"tm": k, "rows": other})
                 send(me != k, outbox.at[layer, g, k, :count], carry.at[layer, g, my_share, :count],
                      car_send.at[g], car_recv.at[layer, g], {"tm": k})
-
-            carry[layer, g, my_share, :count] = outbox[layer, g, me, :count]
+            if part:
+                carry[layer, g, my_share, :count] = outbox[layer, g, me, :count]
+            else:
+                tot[g, :count] = total
+
+        pl.when(is_owner)(gather)
 
     def complete(layer):
         wait_halo(layer, 0)
@@ -280,7 +288,7 @@
             meet()
             for s in range(owners):
                 send(both(me < n - 1, me != base + s), dec_src, dec_box.at[me], dec_send,
-                     dec_recv, {"tm": base + s})
+                     dec_recv.at[late], {"tm": base + s})
             send_fin(layer, 0)
         else:
             w_copies[layer, 0].wait()
@@ -295,9 +303,11 @@
         if layer < layers - 1:
             w_copies[layer + 1, 0].start()
             w_copies[layer + 1, 1].start()
+        for g in range(2):
+            own(layer, g, 0)
         complete(layer)
         for g in range(2):
-            own(layer, g)
+            own(layer, g, 1)
         for g in range(2):
             finish(layer, g)
         finish_halo(layer)
@@ -356,6 +366,7 @@
             pltpu.VMEM((layers, 2, owners, most + 1, 2 * share, chans // 2), BF16),
             pltpu.VMEM((layers, 2, n, most, 2 * share, chans // 2), BF16),
             pltpu.VMEM((layers, 2, n, 2 * share, chans // 2), BF16),
+            pltpu.VMEM((2, most, share, chans), F32),
             pltpu.VMEM((layers, 2, n, most, 2 * share, chans // 2), BF16),
             pltpu.VMEM((layers, 2, owners, most, 2 * share, chans // 2), BF16),
             pltpu.VMEM((layers, 2, owners, 2 * share, chans // 2), BF16),
@@ -365,11 +376,11 @@
             dma((2,)),
             dma((layers, 2, 2)),
             dma,
-            dma,
-            dma((2,)),
-            dma((layers, 2)),
-            dma((2,)),
-            dma((layers, 2)),
+            dma((2,)),
+            dma((2,)),
+            dma((layers, 2, 2)),
+            dma((2,)),
+            dma((layers, 2, 2)),
             dma((2,)),
             dma((layers, 2)),
             dma((2,)),

time: 25.1 us -> 25.2 us (level)
  no operation moved by 1% of the time
where the time goes in v4:
time: 25.2 us; the launch traced here: 25 us
  Pallas kernels  24.3 us (96%)
  local copies, waits for them, and re-layouts  0.71 us (3%)
    pallas_call x1, Pallas kernels, per_device(): pl.pallas_call(functools.partial(kernel, n, bands, base, owners), out_sha...  24.3 us
    unnamed x1, local copies, waits for them, and re-layouts  0.71 us

profile of v4, /device:TPU:3, one launch (start us, length us, event | category | flops | bytes accessed | tf_op | source)
XLA Modules:
  0.0 25.0 jit_solution(1949596865204640775)
XLA Ops:
  0.0 24.3 %shard_map.64 = bf16[4,4,32,256]{3,2,1,0:T(8,128)(2,1)S(1)} custom-call(bf16[4,4,32,256]{3,2,1,0:T(8,128)(2,1)} %lat.1, f32[4]{0:T(128)} %gaps_in.1, f32[2,256]{1,0:T(2,128)} %rates_in.1, f32[2,256]{1,0:T(2,128)} %feed_in.1, bf16[2,3,3,256,256]{4,3,2,1,0:T(8,128)(2,1)} %win.1, bf16[2,3,3,256,256]{4,3,2,1,0:T(8,128)(2,1)} %wout.1), custom_call_target="tpu_custom_call" | custom-call | tf_op jit(solution)/shard_map/pallas_call | solution.py:346
  24.3 0.7 %copy.8 = bf16[4,4,32,256]{3,2,1,0:T(8,128)(2,1)} copy(bf16[4,4,32,256]{3,2,1,0:T(8,128)(2,1)S(1)} %shard_map.64) | data formatting | bytes 524288
